TPU v7x, 512 devices: a whole 4x8x8 slice. The times are simulated.
512 devices in a mesh: group: 64 (over x, y_lo, z), member: 8 (over y_hi, core).
Axes of the slice: x: 4, y: 8 (y_hi: 4, y_lo: 2; y = y_hi * 2 + y_lo), z: 8, core: 2. Of those that a mesh axis runs over, the one named last changes fastest.
Arguments:
- load: float32 [512, 16, 768], P(('group', 'member')), may hold values from -6 to 6
- stiffness: bfloat16 [512, 768, 1024], P(('group', 'member')), as said below
- block_inverse: bfloat16 [512, 768, 1024], P(('group', 'member')), as said below
- deflation: bfloat16 [512, 32, 1024], P(('group', 'member')), may hold values from -0.375 to 0.375
- margin_rows: int32 [512, 4, 64], P(('group', 'member')), may hold values from 0 to 767
- coarse_inverse: bfloat16 [256, 64, 16384], P('member', None, 'group'), as said below
Outputs:
- solution: float32 [512, 16, 768], P(('group', 'member'))
- residual: float32 [512, 16, 768], P(('group', 'member'))
Inputs may be any that keep to these rules, and one draw needn't show every extreme that they name: `margin_rows`: row numbers may repeat within a list. `stiffness`: each row's entry in the column of its own unknown (column i for row i) is the largest entry of the row in magnitude. `block_inverse`: each row's entry in the column of its own unknown is the largest entry of the row in magnitude. `coarse_inverse`: entry [l, h, j] with h * 256 + l == j is the largest entry of its row in magnitude.
All inputs are finite; a program needn't handle non-finite values.
Results may differ from a plain program's by a relative error of at most 0.0085.
Values may be sent and summed in bfloat16 or wider, within the bound.
No kernel may reach another device: no remote copies, remote signals or barrier semaphores. Data moves between devices by JAX's collectives and lax.ppermute only.
A program may use at most 64 MiB of HBM per device.

v0:
```python
import jax
import jax.numpy as jnp
from jax import lax
from jax.sharding import PartitionSpec as P

ITERS = 2


def from_behind(shard, axis, by):
    peers = lax.axis_size(axis)
    return lax.ppermute(shard, axis, [(i, (i + by) % peers) for i in range(peers)])


def local(load, stiffness, block_inverse, deflation, margin_rows, coarse_inverse):
    own_load = load[0]
    stiff_rows = stiffness[0]
    inverse_rows = block_inverse[0]
    basis_rows = deflation[0]
    own_lists = margin_rows[0]
    owned_count = own_load.shape[1]

    def extend(values):
        from_group_lower = from_behind(values, "group", 1)
        from_group_upper = from_behind(values, "group", -1)
        from_member_lower = from_behind(values, "member", 1)
        from_member_upper = from_behind(values, "member", -1)
        pieces = [
            jnp.take(from_group_lower, own_lists[0], axis=1),
            jnp.take(from_group_upper, own_lists[1], axis=1),
            jnp.take(from_member_lower, own_lists[2], axis=1),
            jnp.take(from_member_upper, own_lists[3], axis=1),
        ]
        return jnp.concatenate([values] + pieces, axis=1)

    solution = jnp.zeros_like(own_load)
    residual = own_load
    for step_index in range(ITERS):
        block_values = extend(residual.astype(jnp.bfloat16))
        own_coef = jnp.einsum(
            "cn,kn->ck", block_values, basis_rows, preferred_element_type=jnp.float32
        ).astype(jnp.bfloat16)
        gathered = lax.all_gather(own_coef, "member", axis=1, tiled=True)
        shares = jnp.einsum(
            "lhj,cj->hcl", coarse_inverse, gathered, preferred_element_type=jnp.float32
        )
        arrived = lax.all_to_all(shares, "group", 0, 0, tiled=True)
        prolong = jnp.sum(arrived, axis=0).astype(jnp.bfloat16)
        local_fix = jnp.einsum(
            "cn,un->cu", block_values, inverse_rows, preferred_element_type=jnp.float32
        )
        correction = local_fix + jnp.dot(
            prolong, basis_rows[:, :owned_count], preferred_element_type=jnp.float32
        )
        solution = solution + correction
        solution_block = extend(solution.astype(jnp.bfloat16))
        applied = jnp.einsum(
            "cn,un->cu", solution_block, stiff_rows, preferred_element_type=jnp.float32
        )
        residual = own_load - applied
    return (solution[None], residual[None])


def solution(mesh):
    placed = (
        P(("group", "member"), None, None),
        P(("group", "member"), None, None),
        P(("group", "member"), None, None),
        P(("group", "member"), None, None),
        P(("group", "member"), None, None),
        P("member", None, "group"),
    )
    return jax.shard_map(
        local,
        mesh=mesh,
        in_specs=placed,
        out_specs=(P(("group", "member"), None, None), P(("group", "member"), None, None)),
        check_vma=False,
    )
```

profile of v0, /device:TPU:17, one launch (start us, length us, event | category | flops | bytes accessed | tf_op | source)
XLA Modules:
  0.0 184.7 jit_solution(14538968554219266176)
XLA Ops:
  0.7 1.0 bitcast_convert_fusion
  1.6 2.6 %collective-permute-start.3 = (bf16[16,768]{1,0:T(8,128)(2,1)S(1)}, bf16[16,768]{1,0:T(8,128)(2,1)S(1)}, u32[]{:S(2)}, u32[]{:S(2)}) collective-permute-start(bf16[16,768]{1,0:T(8,128)(2,1)S(1)} %bitcast_convert_fusion), channel_id=1, source_target_pairs={{0,7},{1,0},{2,1},{3,2},{4,3},{5,4},{6,5},{7,6},{8,15},{9,8},{10,9... | collective-permute-start | bytes 73736 | tf_op jit(solution)/shard_map/ppermute | solution.py:11
  4.2 5.3 %collective-permute-start.2 = (bf16[16,768]{1,0:T(8,128)(2,1)S(1)}, bf16[16,768]{1,0:T(8,128)(2,1)S(1)}, u32[]{:S(2)}, u32[]{:S(2)}) collective-permute-start(bf16[16,768]{1,0:T(8,128)(2,1)S(1)} %bitcast_convert_fusion), channel_id=1, source_target_pairs={{0,1},{1,2},{2,3},{3,4},{4,5},{5,6},{6,7},{7,0},{8,9},{9,10},{10,1... | collective-permute-start | bytes 73736 | tf_op jit(solution)/shard_map/ppermute | solution.py:11
  9.5 13.6 %collective-permute-start.1 = (bf16[16,768]{1,0:T(8,128)(2,1)S(1)}, bf16[16,768]{1,0:T(8,128)(2,1)S(1)}, u32[]{:S(2)}, u32[]{:S(2)}) collective-permute-start(bf16[16,768]{1,0:T(8,128)(2,1)S(1)} %bitcast_convert_fusion), channel_id=1, source_target_pairs={{0,504},{8,0},{16,8},{24,16},{32,24},{40,32},{48,40},{56,48},{64,5... | collective-permute-start | bytes 73736 | tf_op jit(solution)/shard_map/ppermute | solution.py:11
  23.2 1.9 %collective-permute-start = (bf16[16,768]{1,0:T(8,128)(2,1)S(1)}, bf16[16,768]{1,0:T(8,128)(2,1)S(1)}, u32[]{:S(2)}, u32[]{:S(2)}) collective-permute-start(bf16[16,768]{1,0:T(8,128)(2,1)S(1)} %bitcast_convert_fusion), channel_id=1, source_target_pairs={{0,8},{8,16},{16,24},{24,32},{32,40},{40,48},{48,56},{56,64},{64,7... | collective-permute-start | bytes 73736 | tf_op jit(solution)/shard_map/ppermute | solution.py:11
  25.1 0.8 compare_and_fusion
  26.1 5.9 %collective-permute-done = bf16[16,768]{1,0:T(8,128)(2,1)S(1)} collective-permute-done((bf16[16,768]{1,0:T(8,128)(2,1)S(1)}, bf16[16,768]{1,0:T(8,128)(2,1)S(1)}, u32[]{:S(2)}, u32[]{:S(2)}) %collective-permute-start) | collective-permute-done | bytes 24608 | tf_op jit(solution)/shard_map/ppermute | solution.py:11
  32.1 0.6 gather_fusion
  33.0 0.6 gather_fusion.1
  33.9 0.6 gather_fusion.2
  34.8 0.6 gather_fusion.3
  35.7 1.0 fusion.29
  36.7 13.9 %all-gather = bf16[8,32,16]{1,2,0:T(8,128)(2,1)S(1)} all-gather(bf16[1,32,16]{1,2,0:T(8,128)(2,1)S(1)} %fusion.29), channel_id=1, replica_groups=mesh['group'=64,'member'=8] {'member'}, dimensions={0}, use_global_device_ids=true | all-gather | bytes 9216 | tf_op jit(solution)/shard_map/all_gather | solution.py:42
  50.7 0.5 convolution_bitcast_fusion.1
  51.8 13.7 %all_to_all.10 = f32[64,1,512]{2,1,0:T(1,128)S(1)} all-to-all(f32[64,1,512]{2,1,0:T(1,128)S(1)} %reshape.201), channel_id=1, replica_groups=mesh['group'=64,'member'=8] {'group'}, dimensions={0} | all-to-all | bytes 262144 | tf_op jit(solution)/shard_map/all_to_all | solution.py:46
  66.0 0.9 reduce
  67.3 1.1 fusion.39
  68.4 2.2 %collective-permute-start.4 = (bf16[16,768]{1,0:T(8,128)(2,1)S(1)}, bf16[16,768]{1,0:T(8,128)(2,1)}, u32[]{:S(2)}, u32[]{:S(2)}) collective-permute-start(bf16[16,768]{1,0:T(8,128)(2,1)S(1)} %get-tuple-element.17), channel_id=1, source_target_pairs={{0,8},{8,16},{16,24},{24,32},{32,40},{40,48},{48,56},{56,64},{64,7... | collective-permute-start | bytes 73736 | tf_op jit(solution)/shard_map/ppermute | solution.py:11
  70.7 3.9 %collective-permute-start.7 = (bf16[16,768]{1,0:T(8,128)(2,1)S(1)}, bf16[16,768]{1,0:T(8,128)(2,1)S(1)}, u32[]{:S(2)}, u32[]{:S(2)}) collective-permute-start(bf16[16,768]{1,0:T(8,128)(2,1)S(1)} %get-tuple-element.17), channel_id=1, source_target_pairs={{0,7},{1,0},{2,1},{3,2},{4,3},{5,4},{6,5},{7,6},{8,15},{9,8},{10,9... | collective-permute-start | bytes 73736 | tf_op jit(solution)/shard_map/ppermute | solution.py:11
  74.6 4.0 %collective-permute-start.6 = (bf16[16,768]{1,0:T(8,128)(2,1)S(1)}, bf16[16,768]{1,0:T(8,128)(2,1)S(1)}, u32[]{:S(2)}, u32[]{:S(2)}) collective-permute-start(bf16[16,768]{1,0:T(8,128)(2,1)S(1)} %get-tuple-element.17), channel_id=1, source_target_pairs={{0,1},{1,2},{2,3},{3,4},{4,5},{5,6},{6,7},{7,0},{8,9},{9,10},{10,1... | collective-permute-start | bytes 73736 | tf_op jit(solution)/shard_map/ppermute | solution.py:11
  78.6 7.1 %collective-permute-start.5 = (bf16[16,768]{1,0:T(8,128)(2,1)S(1)}, bf16[16,768]{1,0:T(8,128)(2,1)}, u32[]{:S(2)}, u32[]{:S(2)}) collective-permute-start(bf16[16,768]{1,0:T(8,128)(2,1)S(1)} %get-tuple-element.17), channel_id=1, source_target_pairs={{0,504},{8,0},{16,8},{24,16},{32,24},{40,32},{48,40},{56,48},{64,5... | collective-permute-start | bytes 73736 | tf_op jit(solution)/shard_map/ppermute | solution.py:11
  85.7 0.9 copy.84
  86.6 0.6 gather_fusion.4
  87.3 0.9 copy.86
  88.2 0.8 gather_fusion.5
  89.1 0.6 select_bitcast_fusion.10
  89.9 0.8 gather_fusion.6
  90.7 0.7 select_bitcast_fusion.9
  91.6 0.8 gather_fusion.7
  92.4 0.6 select_bitcast_fusion.8
  93.2 0.5 fusion.26
  93.7 1.9 %collective-permute-start.8 = (bf16[16,768]{1,0:T(8,128)(2,1)S(1)}, bf16[16,768]{1,0:T(8,128)(2,1)}, u32[]{:S(2)}, u32[]{:S(2)}) collective-permute-start(bf16[16,768]{1,0:T(8,128)(2,1)S(1)} %fusion.26), channel_id=1, source_target_pairs={{0,8},{8,16},{16,24},{24,32},{32,40},{40,48},{48,56},{56,64},{64,7... | collective-permute-start | bytes 73736 | tf_op jit(solution)/shard_map/ppermute | solution.py:11
  95.6 1.9 %collective-permute-start.11 = (bf16[16,768]{1,0:T(8,128)(2,1)S(1)}, bf16[16,768]{1,0:T(8,128)(2,1)S(1)}, u32[]{:S(2)}, u32[]{:S(2)}) collective-permute-start(bf16[16,768]{1,0:T(8,128)(2,1)S(1)} %fusion.26), channel_id=1, source_target_pairs={{0,7},{1,0},{2,1},{3,2},{4,3},{5,4},{6,5},{7,6},{8,15},{9,8},{10,9... | collective-permute-start | bytes 73736 | tf_op jit(solution)/shard_map/ppermute | solution.py:11
  97.5 5.8 %collective-permute-start.10 = (bf16[16,768]{1,0:T(8,128)(2,1)S(1)}, bf16[16,768]{1,0:T(8,128)(2,1)S(1)}, u32[]{:S(2)}, u32[]{:S(2)}) collective-permute-start(bf16[16,768]{1,0:T(8,128)(2,1)S(1)} %fusion.26), channel_id=1, source_target_pairs={{0,1},{1,2},{2,3},{3,4},{4,5},{5,6},{6,7},{7,0},{8,9},{9,10},{10,1... | collective-permute-start | bytes 73736 | tf_op jit(solution)/shard_map/ppermute | solution.py:11
  103.3 7.6 %collective-permute-start.9 = (bf16[16,768]{1,0:T(8,128)(2,1)S(1)}, bf16[16,768]{1,0:T(8,128)(2,1)}, u32[]{:S(2)}, u32[]{:S(2)}) collective-permute-start(bf16[16,768]{1,0:T(8,128)(2,1)S(1)} %fusion.26), channel_id=1, source_target_pairs={{0,504},{8,0},{16,8},{24,16},{32,24},{40,32},{48,40},{56,48},{64,5... | collective-permute-start | bytes 73736 | tf_op jit(solution)/shard_map/ppermute | solution.py:11
  110.9 0.9 copy.92
  111.8 0.8 gather_fusion.8
  112.7 0.9 copy.94
  113.6 0.8 gather_fusion.9
  114.4 0.6 select_bitcast_fusion.6
  115.2 0.8 gather_fusion.10
  116.1 0.7 select_bitcast_fusion.5
  116.9 0.8 gather_fusion.11
  117.8 0.6 select_bitcast_fusion.4
  118.6 11.8 %all-gather.1 = bf16[8,32,16]{1,2,0:T(8,128)(2,1)S(1)} all-gather(bf16[1,32,16]{1,2,0:T(8,128)(2,1)S(1)} %fusion.30), channel_id=1, replica_groups=mesh['group'=64,'member'=8] {'member'}, dimensions={0}, use_global_device_ids=true | all-gather | bytes 9216 | tf_op jit(solution)/shard_map/all_gather | solution.py:42
  130.5 0.7 reshape.198
  131.1 1.7 convolution_bitcast_fusion
  132.9 1.1 copy.101
  134.0 1.3 reshape.203
  135.3 17.8 %all_to_all.11 = f32[64,1,512]{2,1,0:T(1,128)S(1)} all-to-all(f32[64,1,512]{2,1,0:T(1,128)S(1)} %reshape.203), channel_id=1, replica_groups=mesh['group'=64,'member'=8] {'group'}, dimensions={0} | all-to-all | bytes 262144 | tf_op jit(solution)/shard_map/all_to_all | solution.py:46
  153.1 0.9 reduce.1
  153.9 1.0 reshape.204
  154.9 1.1 reduce_sum.19
  156.2 1.9 %fusion.40 = (bf16[16,768]{1,0:T(8,128)(2,1)S(1)}, f32[16,768]{1,0:T(8,128)}) fusion(f32[16,768]{1,0:T(8,128)} %get-tuple-element.18, f32[16,768]{1,0:T(8,128)S(1)} %fusion.31, bf16[16,1024]{1,0:T(8,128)(2,1)S(1)} %concatenate.14, bf16[1,768,1024]{2,1,0:T(8,128)(2,1)S(1)} %copy-done), kind=kOutput, calls=%fused_computation.75 | convolution fusion | flops 25202688 | bytes 1777664 | tf_op jit(solution)/shard_map/cn,un->cu/dot_general | solution.py:48
  158.1 2.5 %collective-permute-start.12 = (bf16[16,768]{1,0:T(8,128)(2,1)S(1)}, bf16[16,768]{1,0:T(8,128)(2,1)S(1)}, u32[]{:S(2)}, u32[]{:S(2)}) collective-permute-start(bf16[16,768]{1,0:T(8,128)(2,1)S(1)} %get-tuple-element.19), channel_id=1, source_target_pairs={{0,8},{8,16},{16,24},{24,32},{32,40},{40,48},{48,56},{56,64},{64,7... | collective-permute-start | bytes 73736 | tf_op jit(solution)/shard_map/ppermute | solution.py:11
  160.6 7.0 %collective-permute-start.13 = (bf16[16,768]{1,0:T(8,128)(2,1)S(1)}, bf16[16,768]{1,0:T(8,128)(2,1)S(1)}, u32[]{:S(2)}, u32[]{:S(2)}) collective-permute-start(bf16[16,768]{1,0:T(8,128)(2,1)S(1)} %get-tuple-element.19), channel_id=1, source_target_pairs={{0,504},{8,0},{16,8},{24,16},{32,24},{40,32},{48,40},{56,48},{64,5... | collective-permute-start | bytes 73736 | tf_op jit(solution)/shard_map/ppermute | solution.py:11
  167.6 7.5 %collective-permute-start.14 = (bf16[16,768]{1,0:T(8,128)(2,1)S(1)}, bf16[16,768]{1,0:T(8,128)(2,1)S(1)}, u32[]{:S(2)}, u32[]{:S(2)}) collective-permute-start(bf16[16,768]{1,0:T(8,128)(2,1)S(1)} %get-tuple-element.19), channel_id=1, source_target_pairs={{0,1},{1,2},{2,3},{3,4},{4,5},{5,6},{6,7},{7,0},{8,9},{9,10},{10,1... | collective-permute-start | bytes 73736 | tf_op jit(solution)/shard_map/ppermute | solution.py:11
  175.1 1.9 %collective-permute-start.15 = (bf16[16,768]{1,0:T(8,128)(2,1)S(1)}, bf16[16,768]{1,0:T(8,128)(2,1)S(1)}, u32[]{:S(2)}, u32[]{:S(2)}) collective-permute-start(bf16[16,768]{1,0:T(8,128)(2,1)S(1)} %get-tuple-element.19), channel_id=1, source_target_pairs={{0,7},{1,0},{2,1},{3,2},{4,3},{5,4},{6,5},{7,6},{8,15},{9,8},{10,9... | collective-permute-start | bytes 73736 | tf_op jit(solution)/shard_map/ppermute | solution.py:11
  177.2 0.8 gather_fusion.12
  178.3 0.8 gather_fusion.13
  179.3 0.8 gather_fusion.14
  180.1 2.3 %collective-permute-done.15 = bf16[16,768]{1,0:T(8,128)(2,1)S(1)} collective-permute-done((bf16[16,768]{1,0:T(8,128)(2,1)S(1)}, bf16[16,768]{1,0:T(8,128)(2,1)S(1)}, u32[]{:S(2)}, u32[]{:S(2)}) %collective-permute-start.15) | collective-permute-done | bytes 24608 | tf_op jit(solution)/shard_map/ppermute | solution.py:11
  182.6 0.8 gather_fusion.15
  183.5 1.1 fusion.23
  (105 shorter events, 5.6 us)
Async XLA Ops:
  0.6 66.6 %copy-start = (bf16[1,768,1024]{2,1,0:T(8,128)(2,1)S(1)}, bf16[1,768,1024]{2,1,0:T(8,128)(2,1)}, u32[]{:S(2)}) copy-start(bf16[1,768,1024]{2,1,0:T(8,128)(2,1)} %param.10) | copy-start | bytes 4718596
  0.6 50.0 %copy-start.2 = (bf16[32,64,256]{2,1,0:T(8,128)(2,1)S(1)}, bf16[32,64,256]{2,1,0:T(8,128)(2,1)}, u32[]{:S(2)}) copy-start(bf16[32,64,256]{2,1,0:T(8,128)(2,1)} %param.13) | copy-start | bytes 3145732
  1.6 33.0 %collective-permute-start.3 = (bf16[16,768]{1,0:T(8,128)(2,1)S(1)}, bf16[16,768]{1,0:T(8,128)(2,1)S(1)}, u32[]{:S(2)}, u32[]{:S(2)}) collective-permute-start(bf16[16,768]{1,0:T(8,128)(2,1)S(1)} %bitcast_convert_fusion), channel_id=1, source_target_pairs={{0,7},{1,0},{2,1},{3,2},{4,3},{5,4},{6,5},{7,6},{8,15},{9,8},{10,9... | collective-permute-start | bytes 73736 | tf_op jit(solution)/shard_map/ppermute | solution.py:11
  4.2 29.6 %collective-permute-start.2 = (bf16[16,768]{1,0:T(8,128)(2,1)S(1)}, bf16[16,768]{1,0:T(8,128)(2,1)S(1)}, u32[]{:S(2)}, u32[]{:S(2)}) collective-permute-start(bf16[16,768]{1,0:T(8,128)(2,1)S(1)} %bitcast_convert_fusion), channel_id=1, source_target_pairs={{0,1},{1,2},{2,3},{3,4},{4,5},{5,6},{6,7},{7,0},{8,9},{9,10},{10,1... | collective-permute-start | bytes 73736 | tf_op jit(solution)/shard_map/ppermute | solution.py:11
  9.5 23.3 %collective-permute-start.1 = (bf16[16,768]{1,0:T(8,128)(2,1)S(1)}, bf16[16,768]{1,0:T(8,128)(2,1)S(1)}, u32[]{:S(2)}, u32[]{:S(2)}) collective-permute-start(bf16[16,768]{1,0:T(8,128)(2,1)S(1)} %bitcast_convert_fusion), channel_id=1, source_target_pairs={{0,504},{8,0},{16,8},{24,16},{32,24},{40,32},{48,40},{56,48},{64,5... | collective-permute-start | bytes 73736 | tf_op jit(solution)/shard_map/ppermute | solution.py:11
  23.2 8.8 %collective-permute-start = (bf16[16,768]{1,0:T(8,128)(2,1)S(1)}, bf16[16,768]{1,0:T(8,128)(2,1)S(1)}, u32[]{:S(2)}, u32[]{:S(2)}) collective-permute-start(bf16[16,768]{1,0:T(8,128)(2,1)S(1)} %bitcast_convert_fusion), channel_id=1, source_target_pairs={{0,8},{8,16},{16,24},{24,32},{32,40},{40,48},{48,56},{56,64},{64,7... | collective-permute-start | bytes 73736 | tf_op jit(solution)/shard_map/ppermute | solution.py:11
  25.9 25.6 %copy-start.5 = (pred[64]{0:T(512)(128)(4,1)}, pred[64]{0:T(512)(128)(4,1)S(1)}, u32[]{:S(2)}) copy-start(pred[64]{0:T(512)(128)(4,1)S(1)} %get-tuple-element.3) | copy-start | bytes 196
  26.0 25.6 %copy-start.7 = (pred[64]{0:T(512)(128)(4,1)}, pred[64]{0:T(512)(128)(4,1)S(1)}, u32[]{:S(2)}) copy-start(pred[64]{0:T(512)(128)(4,1)S(1)} %get-tuple-element.15) | copy-start | bytes 196
  26.0 25.6 %copy-start.9 = (pred[64]{0:T(512)(128)(4,1)}, pred[64]{0:T(512)(128)(4,1)S(1)}, u32[]{:S(2)}) copy-start(pred[64]{0:T(512)(128)(4,1)S(1)} %get-tuple-element.11) | copy-start | bytes 196
  26.0 61.3 %copy-start.11 = (pred[64]{0:T(512)(128)(4,1)}, pred[64]{0:T(512)(128)(4,1)S(1)}, u32[]{:S(2)}) copy-start(pred[64]{0:T(512)(128)(4,1)S(1)} %get-tuple-element.13) | copy-start | bytes 196
  26.0 25.6 %copy-start.14 = (s32[1024]{0:T(1024)}, s32[1024]{0:T(1024)S(1)}, u32[]{:S(2)}) copy-start(s32[1024]{0:T(1024)S(1)} %pad_clamp_fusion) | copy-start | bytes 12292
  26.0 25.5 %copy-start.16 = (s32[1024]{0:T(1024)}, s32[1024]{0:T(1024)S(1)}, u32[]{:S(2)}) copy-start(s32[1024]{0:T(1024)S(1)} %pad_clamp_fusion.2) | copy-start | bytes 12292
  26.0 60.5 %copy-start.17 = (s32[1024]{0:T(1024)}, s32[1024]{0:T(1024)S(1)}, u32[]{:S(2)}) copy-start(s32[1024]{0:T(1024)S(1)} %pad_clamp_fusion.3) | copy-start | bytes 12292
  26.1 25.5 %copy-start.15 = (s32[1024]{0:T(1024)}, s32[1024]{0:T(1024)S(1)}, u32[]{:S(2)}) copy-start(s32[1024]{0:T(1024)S(1)} %pad_clamp_fusion.1) | copy-start | bytes 12292
  51.2 15.9 %copy-start.3 = (bf16[1,32,1024]{2,1,0:T(8,128)(2,1)S(1)}, bf16[1,32,1024]{2,1,0:T(8,128)(2,1)}, u32[]{:S(2)}) copy-start(bf16[1,32,1024]{2,1,0:T(8,128)(2,1)} %param.11) | copy-start | bytes 196612
  67.1 26.0 %copy-start.1 = (bf16[1,768,1024]{2,1,0:T(8,128)(2,1)S(1)}, bf16[1,768,1024]{2,1,0:T(8,128)(2,1)}, u32[]{:S(2)}) copy-start(bf16[1,768,1024]{2,1,0:T(8,128)(2,1)} %param.9) | copy-start | bytes 4718596
  67.1 26.0 %copy-start.4 = (f32[1,16,768]{2,1,0:T(8,128)S(1)}, f32[1,16,768]{2,1,0:T(8,128)}, u32[]{:S(2)}) copy-start(f32[1,16,768]{2,1,0:T(8,128)} %param.8) | copy-start | bytes 147460
  68.4 17.3 %collective-permute-start.4 = (bf16[16,768]{1,0:T(8,128)(2,1)S(1)}, bf16[16,768]{1,0:T(8,128)(2,1)}, u32[]{:S(2)}, u32[]{:S(2)}) collective-permute-start(bf16[16,768]{1,0:T(8,128)(2,1)S(1)} %get-tuple-element.17), channel_id=1, source_target_pairs={{0,8},{8,16},{16,24},{24,32},{32,40},{40,48},{48,56},{56,64},{64,7... | collective-permute-start | bytes 73736 | tf_op jit(solution)/shard_map/ppermute | solution.py:11
  70.7 20.8 %collective-permute-start.7 = (bf16[16,768]{1,0:T(8,128)(2,1)S(1)}, bf16[16,768]{1,0:T(8,128)(2,1)S(1)}, u32[]{:S(2)}, u32[]{:S(2)}) collective-permute-start(bf16[16,768]{1,0:T(8,128)(2,1)S(1)} %get-tuple-element.17), channel_id=1, source_target_pairs={{0,7},{1,0},{2,1},{3,2},{4,3},{5,4},{6,5},{7,6},{8,15},{9,8},{10,9... | collective-permute-start | bytes 73736 | tf_op jit(solution)/shard_map/ppermute | solution.py:11
  74.6 15.1 %collective-permute-start.6 = (bf16[16,768]{1,0:T(8,128)(2,1)S(1)}, bf16[16,768]{1,0:T(8,128)(2,1)S(1)}, u32[]{:S(2)}, u32[]{:S(2)}) collective-permute-start(bf16[16,768]{1,0:T(8,128)(2,1)S(1)} %get-tuple-element.17), channel_id=1, source_target_pairs={{0,1},{1,2},{2,3},{3,4},{4,5},{5,6},{6,7},{7,0},{8,9},{9,10},{10,1... | collective-permute-start | bytes 73736 | tf_op jit(solution)/shard_map/ppermute | solution.py:11
  78.6 8.7 %collective-permute-start.5 = (bf16[16,768]{1,0:T(8,128)(2,1)S(1)}, bf16[16,768]{1,0:T(8,128)(2,1)}, u32[]{:S(2)}, u32[]{:S(2)}) collective-permute-start(bf16[16,768]{1,0:T(8,128)(2,1)S(1)} %get-tuple-element.17), channel_id=1, source_target_pairs={{0,504},{8,0},{16,8},{24,16},{32,24},{40,32},{48,40},{56,48},{64,5... | collective-permute-start | bytes 73736 | tf_op jit(solution)/shard_map/ppermute | solution.py:11
  93.1 19.5 %copy-start.12 = (pred[64]{0:T(512)(128)(4,1)S(1)}, pred[64]{0:T(512)(128)(4,1)}, u32[]{:S(2)}) copy-start(pred[64]{0:T(512)(128)(4,1)} %copy-done.11) | copy-start | bytes 196
  93.7 17.2 %collective-permute-start.8 = (bf16[16,768]{1,0:T(8,128)(2,1)S(1)}, bf16[16,768]{1,0:T(8,128)(2,1)}, u32[]{:S(2)}, u32[]{:S(2)}) collective-permute-start(bf16[16,768]{1,0:T(8,128)(2,1)S(1)} %fusion.26), channel_id=1, source_target_pairs={{0,8},{8,16},{16,24},{24,32},{32,40},{40,48},{48,56},{56,64},{64,7... | collective-permute-start | bytes 73736 | tf_op jit(solution)/shard_map/ppermute | solution.py:11
  95.6 21.2 %collective-permute-start.11 = (bf16[16,768]{1,0:T(8,128)(2,1)S(1)}, bf16[16,768]{1,0:T(8,128)(2,1)S(1)}, u32[]{:S(2)}, u32[]{:S(2)}) collective-permute-start(bf16[16,768]{1,0:T(8,128)(2,1)S(1)} %fusion.26), channel_id=1, source_target_pairs={{0,7},{1,0},{2,1},{3,2},{4,3},{5,4},{6,5},{7,6},{8,15},{9,8},{10,9... | collective-permute-start | bytes 73736 | tf_op jit(solution)/shard_map/ppermute | solution.py:11
  97.5 17.5 %collective-permute-start.10 = (bf16[16,768]{1,0:T(8,128)(2,1)S(1)}, bf16[16,768]{1,0:T(8,128)(2,1)S(1)}, u32[]{:S(2)}, u32[]{:S(2)}) collective-permute-start(bf16[16,768]{1,0:T(8,128)(2,1)S(1)} %fusion.26), channel_id=1, source_target_pairs={{0,1},{1,2},{2,3},{3,4},{4,5},{5,6},{6,7},{7,0},{8,9},{9,10},{10,1... | collective-permute-start | bytes 73736 | tf_op jit(solution)/shard_map/ppermute | solution.py:11
  103.3 9.4 %collective-permute-start.9 = (bf16[16,768]{1,0:T(8,128)(2,1)S(1)}, bf16[16,768]{1,0:T(8,128)(2,1)}, u32[]{:S(2)}, u32[]{:S(2)}) collective-permute-start(bf16[16,768]{1,0:T(8,128)(2,1)S(1)} %fusion.26), channel_id=1, source_target_pairs={{0,504},{8,0},{16,8},{24,16},{32,24},{40,32},{48,40},{56,48},{64,5... | collective-permute-start | bytes 73736 | tf_op jit(solution)/shard_map/ppermute | solution.py:11
  156.0 27.4 %copy-start.10 = (pred[64]{0:T(512)(128)(4,1)S(1)}, pred[64]{0:T(512)(128)(4,1)}, u32[]{:S(2)}) copy-start(pred[64]{0:T(512)(128)(4,1)} %copy-done.9) | copy-start | bytes 196
  156.0 27.4 %copy-start.13 = (pred[64]{0:T(512)(128)(4,1)S(1)}, pred[64]{0:T(512)(128)(4,1)}, u32[]{:S(2)}) copy-start(pred[64]{0:T(512)(128)(4,1)} %copy-done.11) | copy-start | bytes 196
  156.1 27.4 %copy-start.6 = (pred[64]{0:T(512)(128)(4,1)S(1)}, pred[64]{0:T(512)(128)(4,1)}, u32[]{:S(2)}) copy-start(pred[64]{0:T(512)(128)(4,1)} %copy-done.5) | copy-start | bytes 196
  156.1 27.4 %copy-start.8 = (pred[64]{0:T(512)(128)(4,1)S(1)}, pred[64]{0:T(512)(128)(4,1)}, u32[]{:S(2)}) copy-start(pred[64]{0:T(512)(128)(4,1)} %copy-done.7) | copy-start | bytes 196
  158.1 18.9 %collective-permute-start.12 = (bf16[16,768]{1,0:T(8,128)(2,1)S(1)}, bf16[16,768]{1,0:T(8,128)(2,1)S(1)}, u32[]{:S(2)}, u32[]{:S(2)}) collective-permute-start(bf16[16,768]{1,0:T(8,128)(2,1)S(1)} %get-tuple-element.19), channel_id=1, source_target_pairs={{0,8},{8,16},{16,24},{24,32},{32,40},{40,48},{48,56},{56,64},{64,7... | collective-permute-start | bytes 73736 | tf_op jit(solution)/shard_map/ppermute | solution.py:11
  160.6 17.4 %collective-permute-start.13 = (bf16[16,768]{1,0:T(8,128)(2,1)S(1)}, bf16[16,768]{1,0:T(8,128)(2,1)S(1)}, u32[]{:S(2)}, u32[]{:S(2)}) collective-permute-start(bf16[16,768]{1,0:T(8,128)(2,1)S(1)} %get-tuple-element.19), channel_id=1, source_target_pairs={{0,504},{8,0},{16,8},{24,16},{32,24},{40,32},{48,40},{56,48},{64,5... | collective-permute-start | bytes 73736 | tf_op jit(solution)/shard_map/ppermute | solution.py:11
  167.6 11.5 %collective-permute-start.14 = (bf16[16,768]{1,0:T(8,128)(2,1)S(1)}, bf16[16,768]{1,0:T(8,128)(2,1)S(1)}, u32[]{:S(2)}, u32[]{:S(2)}) collective-permute-start(bf16[16,768]{1,0:T(8,128)(2,1)S(1)} %get-tuple-element.19), channel_id=1, source_target_pairs={{0,1},{1,2},{2,3},{3,4},{4,5},{5,6},{6,7},{7,0},{8,9},{9,10},{10,1... | collective-permute-start | bytes 73736 | tf_op jit(solution)/shard_map/ppermute | solution.py:11
  175.1 7.3 %collective-permute-start.15 = (bf16[16,768]{1,0:T(8,128)(2,1)S(1)}, bf16[16,768]{1,0:T(8,128)(2,1)S(1)}, u32[]{:S(2)}, u32[]{:S(2)}) collective-permute-start(bf16[16,768]{1,0:T(8,128)(2,1)S(1)} %get-tuple-element.19), channel_id=1, source_target_pairs={{0,7},{1,0},{2,1},{3,2},{4,3},{5,4},{6,5},{7,6},{8,15},{9,8},{10,9... | collective-permute-start | bytes 73736 | tf_op jit(solution)/shard_map/ppermute | solution.py:11
where the time goes:
time: 186 us; the launch traced here: 185 us
  starting transfers between devices  76.7 us (41%)
  blocking collectives  57.2 us (31%)
  local copies, waits for them, and re-layouts  24.3 us (13%)
  other arithmetic  8.75 us (5%)
  matrix products  8.35 us (4%)
  waiting for transfers between devices  8.18 us (4%)
    ppermute x16, starting transfers between devices, from_behind(): lax.ppermute(shard, axis, [(i, (i + by) % peers) for i in range(peers)])  76.7 us
    all_to_all x2, blocking collectives, local(): arrived = lax.all_to_all(shares, 'group', 0, 0, tiled=True)  31.4 us
    all_gather x2, blocking collectives, local(): gathered = lax.all_gather(own_coef, 'member', axis=1, tiled=True)  25.7 us
    ppermute x16, waiting for transfers between devices, from_behind(): lax.ppermute(shard, axis, [(i, (i + by) % peers) for i in range(peers)])  8.18 us
    ppermute x16, local copies, waits for them, and re-layouts, from_behind(): lax.ppermute(shard, axis, [(i, (i + by) % peers) for i in range(peers)])  5.63 us
  transfers between devices with their start and end apart: 16, of which 2 were waited for; matrix products, arithmetic and copies ran while one was open for 10% of the time, Pallas kernels for 0%

commit v1 on v0

--- a/solution.py
+++ b/solution.py
@@ -39,7 +39,15 @@
         own_coef = jnp.einsum(
             "cn,kn->ck", block_values, basis_rows, preferred_element_type=jnp.float32
         ).astype(jnp.bfloat16)
-        gathered = lax.all_gather(own_coef, "member", axis=1, tiled=True)
+        gathered = jnp.concatenate(
+            jax.lax.all_to_all(
+                jnp.stack([own_coef] * jax.lax.axis_size("member")),
+                "member",
+                split_axis=0,
+                concat_axis=0,
+            ),
+            axis=1,
+        )
         shares = jnp.einsum(
             "lhj,cj->hcl", coarse_inverse, gathered, preferred_element_type=jnp.float32
         )

time: 186 us -> 179 us (0.962)
  the two profiles are of different devices: /device:TPU:17 before, /device:TPU:1 now
where the time goes in v1:
time: 179 us; the launch traced here: 177 us
  starting transfers between devices  71.5 us (40%)
  blocking collectives  55.8 us (31%)
  local copies, waits for them, and re-layouts  24.7 us (14%)
  other arithmetic  8.75 us (5%)
  matrix products  8.35 us (5%)
  waiting for transfers between devices  6.99 us (4%)
    ppermute x16, starting transfers between devices, from_behind(): lax.ppermute(shard, axis, [(i, (i + by) % peers) for i in range(peers)])  71.5 us
    all_to_all x2, blocking collectives, local(): arrived = lax.all_to_all(shares, 'group', 0, 0, tiled=True)  30.3 us
    all_to_all x2, blocking collectives, local(): jax.lax.all_to_all(jnp.stack([own_coef] * jax.lax.axis_size('member')), '...  25.5 us
    ppermute x16, waiting for transfers between devices, from_behind(): lax.ppermute(shard, axis, [(i, (i + by) % peers) for i in range(peers)])  6.99 us
    ppermute x16, local copies, waits for them, and re-layouts, from_behind(): lax.ppermute(shard, axis, [(i, (i + by) % peers) for i in range(peers)])  5.63 us
  transfers between devices with their start and end apart: 16, of which 2 were waited for; matrix products, arithmetic and copies ran while one was open for 10% of the time, Pallas kernels for 0%

profile of v1, /device:TPU:1, one launch (start us, length us, event | category | flops | bytes accessed | tf_op | source)
XLA Modules:
  0.0 177.3 jit_solution(16157001726291903450)
XLA Ops:
  0.7 1.0 bitcast_convert_fusion
  1.6 8.7 %collective-permute-start.3 = (bf16[16,768]{1,0:T(8,128)(2,1)S(1)}, bf16[16,768]{1,0:T(8,128)(2,1)S(1)}, u32[]{:S(2)}, u32[]{:S(2)}) collective-permute-start(bf16[16,768]{1,0:T(8,128)(2,1)S(1)} %bitcast_convert_fusion), channel_id=1, source_target_pairs={{0,7},{1,0},{2,1},{3,2},{4,3},{5,4},{6,5},{7,6},{8,15},{9,8},{10,9... | collective-permute-start | bytes 73736 | tf_op jit(solution)/shard_map/ppermute | solution.py:11
  10.4 1.9 %collective-permute-start.2 = (bf16[16,768]{1,0:T(8,128)(2,1)S(1)}, bf16[16,768]{1,0:T(8,128)(2,1)S(1)}, u32[]{:S(2)}, u32[]{:S(2)}) collective-permute-start(bf16[16,768]{1,0:T(8,128)(2,1)S(1)} %bitcast_convert_fusion), channel_id=1, source_target_pairs={{0,1},{1,2},{2,3},{3,4},{4,5},{5,6},{6,7},{7,0},{8,9},{9,10},{10,1... | collective-permute-start | bytes 73736 | tf_op jit(solution)/shard_map/ppermute | solution.py:11
  12.3 10.7 %collective-permute-start.1 = (bf16[16,768]{1,0:T(8,128)(2,1)S(1)}, bf16[16,768]{1,0:T(8,128)(2,1)S(1)}, u32[]{:S(2)}, u32[]{:S(2)}) collective-permute-start(bf16[16,768]{1,0:T(8,128)(2,1)S(1)} %bitcast_convert_fusion), channel_id=1, source_target_pairs={{0,504},{8,0},{16,8},{24,16},{32,24},{40,32},{48,40},{56,48},{64,5... | collective-permute-start | bytes 73736 | tf_op jit(solution)/shard_map/ppermute | solution.py:11
  23.0 1.9 %collective-permute-start = (bf16[16,768]{1,0:T(8,128)(2,1)S(1)}, bf16[16,768]{1,0:T(8,128)(2,1)S(1)}, u32[]{:S(2)}, u32[]{:S(2)}) collective-permute-start(bf16[16,768]{1,0:T(8,128)(2,1)S(1)} %bitcast_convert_fusion), channel_id=1, source_target_pairs={{0,8},{8,16},{16,24},{24,32},{32,40},{40,48},{48,56},{56,64},{64,7... | collective-permute-start | bytes 73736 | tf_op jit(solution)/shard_map/ppermute | solution.py:11
  24.9 0.8 compare_and_fusion
  25.9 5.9 %collective-permute-done = bf16[16,768]{1,0:T(8,128)(2,1)S(1)} collective-permute-done((bf16[16,768]{1,0:T(8,128)(2,1)S(1)}, bf16[16,768]{1,0:T(8,128)(2,1)S(1)}, u32[]{:S(2)}, u32[]{:S(2)}) %collective-permute-start) | collective-permute-done | bytes 24608 | tf_op jit(solution)/shard_map/ppermute | solution.py:11
  32.0 0.6 gather_fusion
  32.9 0.6 gather_fusion.1
  33.8 0.6 gather_fusion.2
  34.7 0.6 gather_fusion.3
  35.5 1.0 convolution_convert_fusion.1
  36.6 12.9 %all_to_all.20 = bf16[8,2,256]{2,1,0:T(2,128)(2,1)S(1)} all-to-all(bf16[8,2,256]{2,1,0:T(2,128)(2,1)S(1)} %reshape.217), channel_id=1, replica_groups=mesh['group'=64,'member'=8] {'member'}, dimensions={0} | all-to-all | bytes 16384 | tf_op jit(solution)/shard_map/all_to_all | solution.py:43
  49.7 0.5 convolution_bitcast_fusion.1
  50.9 13.4 %all_to_all.21 = f32[64,1,512]{2,1,0:T(1,128)S(1)} all-to-all(f32[64,1,512]{2,1,0:T(1,128)S(1)} %reshape.219), channel_id=1, replica_groups=mesh['group'=64,'member'=8] {'group'}, dimensions={0} | all-to-all | bytes 262144 | tf_op jit(solution)/shard_map/all_to_all | solution.py:54
  64.8 0.9 reduce
  66.1 1.1 fusion.37
  67.2 2.5 %collective-permute-start.4 = (bf16[16,768]{1,0:T(8,128)(2,1)S(1)}, bf16[16,768]{1,0:T(8,128)(2,1)}, u32[]{:S(2)}, u32[]{:S(2)}) collective-permute-start(bf16[16,768]{1,0:T(8,128)(2,1)S(1)} %get-tuple-element.17), channel_id=1, source_target_pairs={{0,8},{8,16},{16,24},{24,32},{32,40},{40,48},{48,56},{56,64},{64,7... | collective-permute-start | bytes 73736 | tf_op jit(solution)/shard_map/ppermute | solution.py:11
  69.7 4.1 %collective-permute-start.7 = (bf16[16,768]{1,0:T(8,128)(2,1)S(1)}, bf16[16,768]{1,0:T(8,128)(2,1)S(1)}, u32[]{:S(2)}, u32[]{:S(2)}) collective-permute-start(bf16[16,768]{1,0:T(8,128)(2,1)S(1)} %get-tuple-element.17), channel_id=1, source_target_pairs={{0,7},{1,0},{2,1},{3,2},{4,3},{5,4},{6,5},{7,6},{8,15},{9,8},{10,9... | collective-permute-start | bytes 73736 | tf_op jit(solution)/shard_map/ppermute | solution.py:11
  73.9 2.3 %collective-permute-start.6 = (bf16[16,768]{1,0:T(8,128)(2,1)S(1)}, bf16[16,768]{1,0:T(8,128)(2,1)S(1)}, u32[]{:S(2)}, u32[]{:S(2)}) collective-permute-start(bf16[16,768]{1,0:T(8,128)(2,1)S(1)} %get-tuple-element.17), channel_id=1, source_target_pairs={{0,1},{1,2},{2,3},{3,4},{4,5},{5,6},{6,7},{7,0},{8,9},{9,10},{10,1... | collective-permute-start | bytes 73736 | tf_op jit(solution)/shard_map/ppermute | solution.py:11
  76.2 7.1 %collective-permute-start.5 = (bf16[16,768]{1,0:T(8,128)(2,1)S(1)}, bf16[16,768]{1,0:T(8,128)(2,1)}, u32[]{:S(2)}, u32[]{:S(2)}) collective-permute-start(bf16[16,768]{1,0:T(8,128)(2,1)S(1)} %get-tuple-element.17), channel_id=1, source_target_pairs={{0,504},{8,0},{16,8},{24,16},{32,24},{40,32},{48,40},{56,48},{64,5... | collective-permute-start | bytes 73736 | tf_op jit(solution)/shard_map/ppermute | solution.py:11
  83.3 0.9 copy.82
  84.2 0.6 gather_fusion.4
  85.0 0.9 copy.84
  85.9 0.8 gather_fusion.5
  86.7 0.6 select_bitcast_fusion.10
  87.5 0.8 gather_fusion.6
  88.4 0.7 select_bitcast_fusion.9
  89.2 0.8 gather_fusion.7
  90.1 0.6 select_bitcast_fusion.8
  90.8 0.5 fusion.26
  91.3 1.9 %collective-permute-start.8 = (bf16[16,768]{1,0:T(8,128)(2,1)S(1)}, bf16[16,768]{1,0:T(8,128)(2,1)}, u32[]{:S(2)}, u32[]{:S(2)}) collective-permute-start(bf16[16,768]{1,0:T(8,128)(2,1)S(1)} %fusion.26), channel_id=1, source_target_pairs={{0,8},{8,16},{16,24},{24,32},{32,40},{40,48},{48,56},{56,64},{64,7... | collective-permute-start | bytes 73736 | tf_op jit(solution)/shard_map/ppermute | solution.py:11
  93.2 2.1 %collective-permute-start.11 = (bf16[16,768]{1,0:T(8,128)(2,1)S(1)}, bf16[16,768]{1,0:T(8,128)(2,1)S(1)}, u32[]{:S(2)}, u32[]{:S(2)}) collective-permute-start(bf16[16,768]{1,0:T(8,128)(2,1)S(1)} %fusion.26), channel_id=1, source_target_pairs={{0,7},{1,0},{2,1},{3,2},{4,3},{5,4},{6,5},{7,6},{8,15},{9,8},{10,9... | collective-permute-start | bytes 73736 | tf_op jit(solution)/shard_map/ppermute | solution.py:11
  95.3 4.4 %collective-permute-start.10 = (bf16[16,768]{1,0:T(8,128)(2,1)S(1)}, bf16[16,768]{1,0:T(8,128)(2,1)S(1)}, u32[]{:S(2)}, u32[]{:S(2)}) collective-permute-start(bf16[16,768]{1,0:T(8,128)(2,1)S(1)} %fusion.26), channel_id=1, source_target_pairs={{0,1},{1,2},{2,3},{3,4},{4,5},{5,6},{6,7},{7,0},{8,9},{9,10},{10,1... | collective-permute-start | bytes 73736 | tf_op jit(solution)/shard_map/ppermute | solution.py:11
  99.7 7.6 %collective-permute-start.9 = (bf16[16,768]{1,0:T(8,128)(2,1)S(1)}, bf16[16,768]{1,0:T(8,128)(2,1)}, u32[]{:S(2)}, u32[]{:S(2)}) collective-permute-start(bf16[16,768]{1,0:T(8,128)(2,1)S(1)} %fusion.26), channel_id=1, source_target_pairs={{0,504},{8,0},{16,8},{24,16},{32,24},{40,32},{48,40},{56,48},{64,5... | collective-permute-start | bytes 73736 | tf_op jit(solution)/shard_map/ppermute | solution.py:11
  107.3 0.9 copy.90
  108.2 0.8 gather_fusion.8
  109.1 0.9 copy.92
  110.0 0.8 gather_fusion.9
  110.8 0.6 select_bitcast_fusion.6
  111.6 0.8 gather_fusion.10
  112.5 0.7 select_bitcast_fusion.5
  113.3 0.8 gather_fusion.11
  114.2 0.6 select_bitcast_fusion.4
  115.1 12.6 %all_to_all.22 = bf16[8,2,256]{2,1,0:T(2,128)(2,1)S(1)} all-to-all(bf16[8,2,256]{2,1,0:T(2,128)(2,1)S(1)} %reshape.221), channel_id=1, replica_groups=mesh['group'=64,'member'=8] {'member'}, dimensions={0} | all-to-all | bytes 16384 | tf_op jit(solution)/shard_map/all_to_all | solution.py:43
  127.8 0.7 reshape.214
  128.5 1.7 convolution_bitcast_fusion
  130.3 1.1 copy.99
  131.4 1.3 reshape.223
  132.7 16.9 %all_to_all.23 = f32[64,1,512]{2,1,0:T(1,128)S(1)} all-to-all(f32[64,1,512]{2,1,0:T(1,128)S(1)} %reshape.223), channel_id=1, replica_groups=mesh['group'=64,'member'=8] {'group'}, dimensions={0} | all-to-all | bytes 262144 | tf_op jit(solution)/shard_map/all_to_all | solution.py:54
  149.5 0.9 reduce.1
  150.4 1.0 reshape.224
  151.4 1.1 reduce_sum.19
  152.7 1.9 %fusion.38 = (bf16[16,768]{1,0:T(8,128)(2,1)S(1)}, f32[16,768]{1,0:T(8,128)}) fusion(f32[16,768]{1,0:T(8,128)} %get-tuple-element.18, f32[16,768]{1,0:T(8,128)S(1)} %fusion.29, bf16[16,1024]{1,0:T(8,128)(2,1)S(1)} %concatenate.14, bf16[1,768,1024]{2,1,0:T(8,128)(2,1)S(1)} %copy-done), kind=kOutput, calls=%fused_computation.73 | convolution fusion | flops 25202688 | bytes 1777664 | tf_op jit(solution)/shard_map/cn,un->cu/dot_general | solution.py:56
  154.6 2.4 %collective-permute-start.12 = (bf16[16,768]{1,0:T(8,128)(2,1)S(1)}, bf16[16,768]{1,0:T(8,128)(2,1)S(1)}, u32[]{:S(2)}, u32[]{:S(2)}) collective-permute-start(bf16[16,768]{1,0:T(8,128)(2,1)S(1)} %get-tuple-element.19), channel_id=1, source_target_pairs={{0,8},{8,16},{16,24},{24,32},{32,40},{40,48},{48,56},{56,64},{64,7... | collective-permute-start | bytes 73736 | tf_op jit(solution)/shard_map/ppermute | solution.py:11
  157.0 7.1 %collective-permute-start.13 = (bf16[16,768]{1,0:T(8,128)(2,1)S(1)}, bf16[16,768]{1,0:T(8,128)(2,1)S(1)}, u32[]{:S(2)}, u32[]{:S(2)}) collective-permute-start(bf16[16,768]{1,0:T(8,128)(2,1)S(1)} %get-tuple-element.19), channel_id=1, source_target_pairs={{0,504},{8,0},{16,8},{24,16},{32,24},{40,32},{48,40},{56,48},{64,5... | collective-permute-start | bytes 73736 | tf_op jit(solution)/shard_map/ppermute | solution.py:11
  164.1 4.8 %collective-permute-start.14 = (bf16[16,768]{1,0:T(8,128)(2,1)S(1)}, bf16[16,768]{1,0:T(8,128)(2,1)S(1)}, u32[]{:S(2)}, u32[]{:S(2)}) collective-permute-start(bf16[16,768]{1,0:T(8,128)(2,1)S(1)} %get-tuple-element.19), channel_id=1, source_target_pairs={{0,1},{1,2},{2,3},{3,4},{4,5},{5,6},{6,7},{7,0},{8,9},{9,10},{10,1... | collective-permute-start | bytes 73736 | tf_op jit(solution)/shard_map/ppermute | solution.py:11
  168.9 1.9 %collective-permute-start.15 = (bf16[16,768]{1,0:T(8,128)(2,1)S(1)}, bf16[16,768]{1,0:T(8,128)(2,1)S(1)}, u32[]{:S(2)}, u32[]{:S(2)}) collective-permute-start(bf16[16,768]{1,0:T(8,128)(2,1)S(1)} %get-tuple-element.19), channel_id=1, source_target_pairs={{0,7},{1,0},{2,1},{3,2},{4,3},{5,4},{6,5},{7,6},{8,15},{9,8},{10,9... | collective-permute-start | bytes 73736 | tf_op jit(solution)/shard_map/ppermute | solution.py:11
  171.0 0.8 gather_fusion.12
  172.0 0.8 gather_fusion.13
  173.1 0.8 gather_fusion.14
  173.9 1.1 collective-permute-done.15
  175.1 0.8 gather_fusion.15
  176.1 1.1 fusion.23
  (111 shorter events, 6.0 us)
Async XLA Ops:
  0.6 65.5 %copy-start = (bf16[1,768,1024]{2,1,0:T(8,128)(2,1)S(1)}, bf16[1,768,1024]{2,1,0:T(8,128)(2,1)}, u32[]{:S(2)}) copy-start(bf16[1,768,1024]{2,1,0:T(8,128)(2,1)} %param.10) | copy-start | bytes 4718596
  0.6 49.1 %copy-start.2 = (bf16[32,64,256]{2,1,0:T(8,128)(2,1)S(1)}, bf16[32,64,256]{2,1,0:T(8,128)(2,1)}, u32[]{:S(2)}) copy-start(bf16[32,64,256]{2,1,0:T(8,128)(2,1)} %param.13) | copy-start | bytes 3145732
  1.6 32.9 %collective-permute-start.3 = (bf16[16,768]{1,0:T(8,128)(2,1)S(1)}, bf16[16,768]{1,0:T(8,128)(2,1)S(1)}, u32[]{:S(2)}, u32[]{:S(2)}) collective-permute-start(bf16[16,768]{1,0:T(8,128)(2,1)S(1)} %bitcast_convert_fusion), channel_id=1, source_target_pairs={{0,7},{1,0},{2,1},{3,2},{4,3},{5,4},{6,5},{7,6},{8,15},{9,8},{10,9... | collective-permute-start | bytes 73736 | tf_op jit(solution)/shard_map/ppermute | solution.py:11
  10.4 23.2 %collective-permute-start.2 = (bf16[16,768]{1,0:T(8,128)(2,1)S(1)}, bf16[16,768]{1,0:T(8,128)(2,1)S(1)}, u32[]{:S(2)}, u32[]{:S(2)}) collective-permute-start(bf16[16,768]{1,0:T(8,128)(2,1)S(1)} %bitcast_convert_fusion), channel_id=1, source_target_pairs={{0,1},{1,2},{2,3},{3,4},{4,5},{5,6},{6,7},{7,0},{8,9},{9,10},{10,1... | collective-permute-start | bytes 73736 | tf_op jit(solution)/shard_map/ppermute | solution.py:11
  12.3 20.4 %collective-permute-start.1 = (bf16[16,768]{1,0:T(8,128)(2,1)S(1)}, bf16[16,768]{1,0:T(8,128)(2,1)S(1)}, u32[]{:S(2)}, u32[]{:S(2)}) collective-permute-start(bf16[16,768]{1,0:T(8,128)(2,1)S(1)} %bitcast_convert_fusion), channel_id=1, source_target_pairs={{0,504},{8,0},{16,8},{24,16},{32,24},{40,32},{48,40},{56,48},{64,5... | collective-permute-start | bytes 73736 | tf_op jit(solution)/shard_map/ppermute | solution.py:11
  23.0 8.8 %collective-permute-start = (bf16[16,768]{1,0:T(8,128)(2,1)S(1)}, bf16[16,768]{1,0:T(8,128)(2,1)S(1)}, u32[]{:S(2)}, u32[]{:S(2)}) collective-permute-start(bf16[16,768]{1,0:T(8,128)(2,1)S(1)} %bitcast_convert_fusion), channel_id=1, source_target_pairs={{0,8},{8,16},{16,24},{24,32},{32,40},{40,48},{48,56},{56,64},{64,7... | collective-permute-start | bytes 73736 | tf_op jit(solution)/shard_map/ppermute | solution.py:11
  25.8 24.8 %copy-start.5 = (pred[64]{0:T(512)(128)(4,1)}, pred[64]{0:T(512)(128)(4,1)S(1)}, u32[]{:S(2)}) copy-start(pred[64]{0:T(512)(128)(4,1)S(1)} %get-tuple-element.3) | copy-start | bytes 196
  25.8 24.8 %copy-start.7 = (pred[64]{0:T(512)(128)(4,1)}, pred[64]{0:T(512)(128)(4,1)S(1)}, u32[]{:S(2)}) copy-start(pred[64]{0:T(512)(128)(4,1)S(1)} %get-tuple-element.15) | copy-start | bytes 196
  25.8 24.8 %copy-start.9 = (pred[64]{0:T(512)(128)(4,1)}, pred[64]{0:T(512)(128)(4,1)S(1)}, u32[]{:S(2)}) copy-start(pred[64]{0:T(512)(128)(4,1)S(1)} %get-tuple-element.11) | copy-start | bytes 196
  25.8 59.1 %copy-start.11 = (pred[64]{0:T(512)(128)(4,1)}, pred[64]{0:T(512)(128)(4,1)S(1)}, u32[]{:S(2)}) copy-start(pred[64]{0:T(512)(128)(4,1)S(1)} %get-tuple-element.13) | copy-start | bytes 196
  25.8 24.8 %copy-start.14 = (s32[1024]{0:T(1024)}, s32[1024]{0:T(1024)S(1)}, u32[]{:S(2)}) copy-start(s32[1024]{0:T(1024)S(1)} %pad_clamp_fusion) | copy-start | bytes 12292
  25.9 24.8 %copy-start.16 = (s32[1024]{0:T(1024)}, s32[1024]{0:T(1024)S(1)}, u32[]{:S(2)}) copy-start(s32[1024]{0:T(1024)S(1)} %pad_clamp_fusion.2) | copy-start | bytes 12292
  25.9 58.3 %copy-start.17 = (s32[1024]{0:T(1024)}, s32[1024]{0:T(1024)S(1)}, u32[]{:S(2)}) copy-start(s32[1024]{0:T(1024)S(1)} %pad_clamp_fusion.3) | copy-start | bytes 12292
  25.9 24.7 %copy-start.15 = (s32[1024]{0:T(1024)}, s32[1024]{0:T(1024)S(1)}, u32[]{:S(2)}) copy-start(s32[1024]{0:T(1024)S(1)} %pad_clamp_fusion.1) | copy-start | bytes 12292
  50.3 15.7 %copy-start.3 = (bf16[1,32,1024]{2,1,0:T(8,128)(2,1)S(1)}, bf16[1,32,1024]{2,1,0:T(8,128)(2,1)}, u32[]{:S(2)}) copy-start(bf16[1,32,1024]{2,1,0:T(8,128)(2,1)} %param.11) | copy-start | bytes 196612
  65.9 24.9 %copy-start.1 = (bf16[1,768,1024]{2,1,0:T(8,128)(2,1)S(1)}, bf16[1,768,1024]{2,1,0:T(8,128)(2,1)}, u32[]{:S(2)}) copy-start(bf16[1,768,1024]{2,1,0:T(8,128)(2,1)} %param.9) | copy-start | bytes 4718596
  65.9 24.9 %copy-start.4 = (f32[1,16,768]{2,1,0:T(8,128)S(1)}, f32[1,16,768]{2,1,0:T(8,128)}, u32[]{:S(2)}) copy-start(f32[1,16,768]{2,1,0:T(8,128)} %param.8) | copy-start | bytes 147460
  67.2 16.1 %collective-permute-start.4 = (bf16[16,768]{1,0:T(8,128)(2,1)S(1)}, bf16[16,768]{1,0:T(8,128)(2,1)}, u32[]{:S(2)}, u32[]{:S(2)}) collective-permute-start(bf16[16,768]{1,0:T(8,128)(2,1)S(1)} %get-tuple-element.17), channel_id=1, source_target_pairs={{0,8},{8,16},{16,24},{24,32},{32,40},{40,48},{48,56},{56,64},{64,7... | collective-permute-start | bytes 73736 | tf_op jit(solution)/shard_map/ppermute | solution.py:11
  69.7 19.3 %collective-permute-start.7 = (bf16[16,768]{1,0:T(8,128)(2,1)S(1)}, bf16[16,768]{1,0:T(8,128)(2,1)S(1)}, u32[]{:S(2)}, u32[]{:S(2)}) collective-permute-start(bf16[16,768]{1,0:T(8,128)(2,1)S(1)} %get-tuple-element.17), channel_id=1, source_target_pairs={{0,7},{1,0},{2,1},{3,2},{4,3},{5,4},{6,5},{7,6},{8,15},{9,8},{10,9... | collective-permute-start | bytes 73736 | tf_op jit(solution)/shard_map/ppermute | solution.py:11
  73.9 13.5 %collective-permute-start.6 = (bf16[16,768]{1,0:T(8,128)(2,1)S(1)}, bf16[16,768]{1,0:T(8,128)(2,1)S(1)}, u32[]{:S(2)}, u32[]{:S(2)}) collective-permute-start(bf16[16,768]{1,0:T(8,128)(2,1)S(1)} %get-tuple-element.17), channel_id=1, source_target_pairs={{0,1},{1,2},{2,3},{3,4},{4,5},{5,6},{6,7},{7,0},{8,9},{9,10},{10,1... | collective-permute-start | bytes 73736 | tf_op jit(solution)/shard_map/ppermute | solution.py:11
  76.2 8.7 %collective-permute-start.5 = (bf16[16,768]{1,0:T(8,128)(2,1)S(1)}, bf16[16,768]{1,0:T(8,128)(2,1)}, u32[]{:S(2)}, u32[]{:S(2)}) collective-permute-start(bf16[16,768]{1,0:T(8,128)(2,1)S(1)} %get-tuple-element.17), channel_id=1, source_target_pairs={{0,504},{8,0},{16,8},{24,16},{32,24},{40,32},{48,40},{56,48},{64,5... | collective-permute-start | bytes 73736 | tf_op jit(solution)/shard_map/ppermute | solution.py:11
  90.8 18.3 %copy-start.12 = (pred[64]{0:T(512)(128)(4,1)S(1)}, pred[64]{0:T(512)(128)(4,1)}, u32[]{:S(2)}) copy-start(pred[64]{0:T(512)(128)(4,1)} %copy-done.11) | copy-start | bytes 196
  91.3 16.0 %collective-permute-start.8 = (bf16[16,768]{1,0:T(8,128)(2,1)S(1)}, bf16[16,768]{1,0:T(8,128)(2,1)}, u32[]{:S(2)}, u32[]{:S(2)}) collective-permute-start(bf16[16,768]{1,0:T(8,128)(2,1)S(1)} %fusion.26), channel_id=1, source_target_pairs={{0,8},{8,16},{16,24},{24,32},{32,40},{40,48},{48,56},{56,64},{64,7... | collective-permute-start | bytes 73736 | tf_op jit(solution)/shard_map/ppermute | solution.py:11
  93.2 19.9 %collective-permute-start.11 = (bf16[16,768]{1,0:T(8,128)(2,1)S(1)}, bf16[16,768]{1,0:T(8,128)(2,1)S(1)}, u32[]{:S(2)}, u32[]{:S(2)}) collective-permute-start(bf16[16,768]{1,0:T(8,128)(2,1)S(1)} %fusion.26), channel_id=1, source_target_pairs={{0,7},{1,0},{2,1},{3,2},{4,3},{5,4},{6,5},{7,6},{8,15},{9,8},{10,9... | collective-permute-start | bytes 73736 | tf_op jit(solution)/shard_map/ppermute | solution.py:11
  95.3 16.1 %collective-permute-start.10 = (bf16[16,768]{1,0:T(8,128)(2,1)S(1)}, bf16[16,768]{1,0:T(8,128)(2,1)S(1)}, u32[]{:S(2)}, u32[]{:S(2)}) collective-permute-start(bf16[16,768]{1,0:T(8,128)(2,1)S(1)} %fusion.26), channel_id=1, source_target_pairs={{0,1},{1,2},{2,3},{3,4},{4,5},{5,6},{6,7},{7,0},{8,9},{9,10},{10,1... | collective-permute-start | bytes 73736 | tf_op jit(solution)/shard_map/ppermute | solution.py:11
  99.7 9.4 %collective-permute-start.9 = (bf16[16,768]{1,0:T(8,128)(2,1)S(1)}, bf16[16,768]{1,0:T(8,128)(2,1)}, u32[]{:S(2)}, u32[]{:S(2)}) collective-permute-start(bf16[16,768]{1,0:T(8,128)(2,1)S(1)} %fusion.26), channel_id=1, source_target_pairs={{0,504},{8,0},{16,8},{24,16},{32,24},{40,32},{48,40},{56,48},{64,5... | collective-permute-start | bytes 73736 | tf_op jit(solution)/shard_map/ppermute | solution.py:11
  152.5 23.5 %copy-start.10 = (pred[64]{0:T(512)(128)(4,1)S(1)}, pred[64]{0:T(512)(128)(4,1)}, u32[]{:S(2)}) copy-start(pred[64]{0:T(512)(128)(4,1)} %copy-done.9) | copy-start | bytes 196
  152.5 23.5 %copy-start.13 = (pred[64]{0:T(512)(128)(4,1)S(1)}, pred[64]{0:T(512)(128)(4,1)}, u32[]{:S(2)}) copy-start(pred[64]{0:T(512)(128)(4,1)} %copy-done.11) | copy-start | bytes 196
  152.5 23.5 %copy-start.6 = (pred[64]{0:T(512)(128)(4,1)S(1)}, pred[64]{0:T(512)(128)(4,1)}, u32[]{:S(2)}) copy-start(pred[64]{0:T(512)(128)(4,1)} %copy-done.5) | copy-start | bytes 196
  152.5 23.5 %copy-start.8 = (pred[64]{0:T(512)(128)(4,1)S(1)}, pred[64]{0:T(512)(128)(4,1)}, u32[]{:S(2)}) copy-start(pred[64]{0:T(512)(128)(4,1)} %copy-done.7) | copy-start | bytes 196
  154.6 16.2 %collective-permute-start.12 = (bf16[16,768]{1,0:T(8,128)(2,1)S(1)}, bf16[16,768]{1,0:T(8,128)(2,1)S(1)}, u32[]{:S(2)}, u32[]{:S(2)}) collective-permute-start(bf16[16,768]{1,0:T(8,128)(2,1)S(1)} %get-tuple-element.19), channel_id=1, source_target_pairs={{0,8},{8,16},{16,24},{24,32},{32,40},{40,48},{48,56},{56,64},{64,7... | collective-permute-start | bytes 73736 | tf_op jit(solution)/shard_map/ppermute | solution.py:11
  157.0 14.8 %collective-permute-start.13 = (bf16[16,768]{1,0:T(8,128)(2,1)S(1)}, bf16[16,768]{1,0:T(8,128)(2,1)S(1)}, u32[]{:S(2)}, u32[]{:S(2)}) collective-permute-start(bf16[16,768]{1,0:T(8,128)(2,1)S(1)} %get-tuple-element.19), channel_id=1, source_target_pairs={{0,504},{8,0},{16,8},{24,16},{32,24},{40,32},{48,40},{56,48},{64,5... | collective-permute-start | bytes 73736 | tf_op jit(solution)/shard_map/ppermute | solution.py:11
  164.1 8.7 %collective-permute-start.14 = (bf16[16,768]{1,0:T(8,128)(2,1)S(1)}, bf16[16,768]{1,0:T(8,128)(2,1)S(1)}, u32[]{:S(2)}, u32[]{:S(2)}) collective-permute-start(bf16[16,768]{1,0:T(8,128)(2,1)S(1)} %get-tuple-element.19), channel_id=1, source_target_pairs={{0,1},{1,2},{2,3},{3,4},{4,5},{5,6},{6,7},{7,0},{8,9},{9,10},{10,1... | collective-permute-start | bytes 73736 | tf_op jit(solution)/shard_map/ppermute | solution.py:11
  168.9 6.1 %collective-permute-start.15 = (bf16[16,768]{1,0:T(8,128)(2,1)S(1)}, bf16[16,768]{1,0:T(8,128)(2,1)S(1)}, u32[]{:S(2)}, u32[]{:S(2)}) collective-permute-start(bf16[16,768]{1,0:T(8,128)(2,1)S(1)} %get-tuple-element.19), channel_id=1, source_target_pairs={{0,7},{1,0},{2,1},{3,2},{4,3},{5,4},{6,5},{7,6},{8,15},{9,8},{10,9... | collective-permute-start | bytes 73736 | tf_op jit(solution)/shard_map/ppermute | solution.py:11
